TPU v7x, 32 devices: a whole 2x2x4 slice. The times are simulated.
32 devices in a mesh: mode: 8 (over z, y), tm: 4 (over x, core).
Axes of the slice: x: 2, y: 2, z: 4, core: 2. Of those that a mesh axis runs over, the one named last changes fastest.
Arguments:
- support_accel: bfloat16 [512, 2048], P(None, 'tm'), may hold values from -6 to 6
- participation: bfloat16 [2048, 512], P('mode'), may hold values from -0.25 to 0.25
- kernels: float32 [2048, 2048], P('mode'), may hold values from -0.25 to 0.25
- lengths: int32 [2048], P('mode'), may hold values from 1 to 2048, as said below
- mode_shapes: bfloat16 [16384, 2048], P('mode'), may hold values from -0.125 to 0.125
- groups: int32 [16384], P('mode'), may hold values from 0 to 511
Outputs:
- response: bfloat16 [16384, 2048], P('mode', 'tm')
Inputs may be any that keep to these rules, and one draw needn't show every extreme that they name: `lengths`: some mode has exactly 2048 taps in every draw.
All inputs are finite; a program needn't handle non-finite values.
Results may differ from a plain program's by a relative error of at most 0.0033.
Values may be sent and summed in bfloat16 or wider, within the bound.
A program may use at most 64 MiB of HBM per device.

v0:
```python
import jax
import jax.numpy as jnp
from jax import lax
from jax.sharding import PartitionSpec as P


def passed_along(block, axis, distance):
    devices = range(lax.axis_size(axis))
    route = [(i - distance, i) for i in devices if i - distance in devices]
    return lax.ppermute(block, axis, route)


def depthwise(signal, weights):
    flipped = jnp.flip(weights, 1)[:, None, :]
    result = lax.conv_general_dilated(
        signal[None],
        flipped,
        (1,),
        "VALID",
        dimension_numbers=("NCH", "OIH", "NCH"),
        feature_group_count=signal.shape[0],
        precision=lax.Precision.HIGHEST,
    )
    return result[0]


def apply_filter(signal, kernel):
    return depthwise(signal, kernel)


def per_device(support_accel, participation, kernels, lengths, mode_shapes, groups):
    slab_len = support_accel.shape[1]
    tap_count = kernels.shape[1]
    depth_slabs = tap_count // slab_len
    forces = jnp.dot(participation, support_accel, preferred_element_type=jnp.float32)
    alive = jnp.arange(tap_count, dtype=jnp.int32)[None, :] < lengths[:, None]
    masked = jnp.where(alive, kernels, jnp.zeros_like(kernels))
    pieces = [forces]
    for distance in range(1, depth_slabs + 1):
        pieces.insert(0, passed_along(forces, "tm", distance))
    window = jnp.concatenate(pieces, axis=1)
    modal = apply_filter(window[:, 1:], masked).astype(jnp.bfloat16)
    initial = jnp.zeros((mode_shapes.shape[0], slab_len), jnp.float32)
    piece = jax.tree.map(lambda part: lax.all_gather(part, "mode", axis=0, tiled=True), modal)
    columns = lax.slice_in_dim(mode_shapes, 0, piece.shape[0], axis=1)
    summed = initial + jnp.dot(columns, piece, preferred_element_type=jnp.float32)
    ground = jnp.take(support_accel, groups, axis=0).astype(jnp.float32)
    return (summed + ground).astype(jnp.bfloat16)


def solution(mesh):
    placed = (
        P(None, "tm"),
        P("mode", None),
        P("mode", None),
        P("mode"),
        P("mode", None),
        P("mode"),
    )
    return jax.shard_map(
        per_device, mesh=mesh, in_specs=placed, out_specs=P("mode", "tm"), check_vma=False
    )
```

profile of v0, /device:TPU:0, one launch (start us, length us, event | category | flops | bytes accessed | tf_op | source)
XLA Modules:
  0.0 271.4 jit_solution(18268262673586640301)
XLA Ops:
  6.5 0.0 copy-start
  6.5 0.0 all-gather.3.cloned.1.call-start
  6.5 1.0 copy-done
  7.6 1.2 fusion.4
  8.8 1.5 collective-permute-start
  10.3 5.1 %collective-permute-start.1 = (f32[256,512]{1,0:T(8,128)S(1)}, f32[256,512]{1,0:T(8,128)}, u32[]{:S(2)}, u32[]{:S(2)}) collective-permute-start(f32[256,512]{1,0:T(8,128)S(1)} %fusion.4), channel_id=1, source_target_pairs={{0,3},{4,7},{8,11},{12,15},{16,19},{20,23},{24,27},{28,31}} | collective-permute-start | bytes 1572872 | tf_op jit(solution)/shard_map/ppermute | solution.py:10
  15.4 2.1 collective-permute-start.2
  17.5 2.1 collective-permute-start.3
  19.6 1.8 fusion.2
  21.4 11.6 %rev.4 = f32[256,2048]{1,0:T(8,128)} reverse(f32[256,2048]{1,0:T(8,128)S(1)} %fusion.2), dimensions={1} | reverse | bytes 4194304 | tf_op jit(solution)/shard_map/jit(_flip)/rev | solution.py:14
  33.0 6.1 %copy.12 = f32[256,1,2048]{0,1,2:T(1,128)} copy(f32[256,1,2048]{2,0,1:T(8,128)} %bitcast.15) | data formatting | bytes 4194304 | tf_op jit(solution)/shard_map/broadcast_in_dim | solution.py:14
  39.1 0.0 collective-permute-done
  39.1 1.1 constant_dynamic-update-slice_fusion.4
  40.2 0.0 collective-permute-done.1
  40.2 1.1 constant_dynamic-update-slice_fusion.3
  41.3 0.0 collective-permute-done.2
  41.3 1.1 constant_dynamic-update-slice_fusion.2
  42.3 0.0 collective-permute-done.3
  42.4 1.1 constant_dynamic-update-slice_fusion.1
  43.5 0.8 slice_bitcast_fusion
  44.2 4.0 %copy.11 = f32[1,256,2559]{1,0,2:T(1,128)} copy(f32[1,256,2559]{2,1,0:T(8,128)S(1)} %slice_bitcast_fusion) | data formatting | bytes 5240832 | tf_op jit(solution)/shard_map/broadcast_in_dim | solution.py:16
  48.3 0.0 copy-start.1
  48.3 90.9 %convolution_convert_fusion = bf16[1,256,512]{1,0,2:T(2,128)(2,1)} fusion(f32[1,256,2559]{1,0,2:T(1,128)} %copy.11, f32[256,1,2048]{0,1,2:T(1,128)} %copy.12), kind=kOutput, calls=%fused_computation.7 | convolution fusion | flops 3221356544 | bytes 4979712 | tf_op jit(solution)/shard_map/conv_general_dilated | solution.py:15
  139.1 0.0 all-gather.3.cloned.1.call-update
  139.2 0.0 copy-done.1
  139.2 7.5 %gather_fusion = bf16[2048,512]{1,0:T(8,128)(2,1)S(1)} fusion(bf16[512,512]{1,0:T(8,128)(2,1)S(1)} %copy-done, s32[2048]{0:T(1024)S(1)} %fusion.3), kind=kCustom, calls=%fused_computation | custom fusion | bytes 4202496 | tf_op jit(solution)/shard_map/jit(_take)/gather | solution.py:47
  146.7 2.4 copy.14
  149.1 92.8 %all-gather.3.cloned.1.call-done = bf16[1,2048,512]{1,0,2:T(2,128)(2,1)} async-done(((bf16[1,256,512]{1,0,2:T(2,128)(2,1)}), bf16[1,2048,512]{1,0,2:T(2,128)(2,1)}) %all-gather.3.cloned.1.call-update) | async-done | bytes 2097168 | tf_op jit(solution)/shard_map/all_gather | solution.py:44
  241.9 9.0 %copy.13 = bf16[1,2048,512]{2,1,0:T(8,128)(2,1)S(1)} copy(bf16[1,2048,512]{1,0,2:T(2,128)(2,1)} %all-gather.3.cloned.1.call-done) | data formatting | bytes 4194304 | tf_op jit(solution)/shard_map/all_gather | solution.py:44
  250.9 9.7 %fusion = bf16[2048,512]{0,1:T(8,128)(2,1)} fusion(bf16[2048,2048]{1,0:T(8,128)(2,1)} %param.10, bf16[1,2048,512]{2,1,0:T(8,128)(2,1)S(1)} %copy.13, bf16[2048,512]{0,1:T(8,128)(2,1)} %copy.14, pred[2048]{0:T(1024)(128)(4,1)S(1)} %compare_and_fusion), kind=kOutput, calls=%fused_computation.2 | convolution fusion | flops 4299161600 | bytes 14682112 | tf_op jit(solution)/shard_map/dot_general | solution.py:46
  260.6 3.9 %copy.15 = bf16[2048,512]{1,0:T(8,128)(2,1)} copy(bf16[2048,512]{0,1:T(8,128)(2,1)} %fusion) | data formatting | bytes 4194304 | tf_op jit(solution)/shard_map/convert_element_type | solution.py:48
  (3 shorter events, 0.1 us)
Async XLA Ops:
  6.5 1.0 copy-start
  6.5 235.4 %all-gather.3.cloned.1.call-start = ((), (), s32[]{:S(2)}) async-start(), calls=%async_computation | async-start | bytes 4718592 | tf_op jit(solution)/shard_map/all_gather | solution.py:44
  8.8 30.3 %collective-permute-start = (f32[256,512]{1,0:T(8,128)S(1)}, f32[256,512]{1,0:T(8,128)}, u32[]{:S(2)}, u32[]{:S(2)}) collective-permute-start(f32[256,512]{1,0:T(8,128)S(1)} %fusion.4), channel_id=1, source_target_pairs={} | collective-permute-start | bytes 1572872 | tf_op jit(solution)/shard_map/ppermute | solution.py:10
  10.3 29.9 %collective-permute-start.1 = (f32[256,512]{1,0:T(8,128)S(1)}, f32[256,512]{1,0:T(8,128)}, u32[]{:S(2)}, u32[]{:S(2)}) collective-permute-start(f32[256,512]{1,0:T(8,128)S(1)} %fusion.4), channel_id=1, source_target_pairs={{0,3},{4,7},{8,11},{12,15},{16,19},{20,23},{24,27},{28,31}} | collective-permute-start | bytes 1572872 | tf_op jit(solution)/shard_map/ppermute | solution.py:10
  15.4 25.9 %collective-permute-start.2 = (f32[256,512]{1,0:T(8,128)S(1)}, f32[256,512]{1,0:T(8,128)}, u32[]{:S(2)}, u32[]{:S(2)}) collective-permute-start(f32[256,512]{1,0:T(8,128)S(1)} %fusion.4), channel_id=1, source_target_pairs={{0,2},{1,3},{4,6},{5,7},{8,10},{9,11},{12,14},{13,15},{16,18},{17,... | collective-permute-start | bytes 1572872 | tf_op jit(solution)/shard_map/ppermute | solution.py:10
  17.5 24.9 %collective-permute-start.3 = (f32[256,512]{1,0:T(8,128)S(1)}, f32[256,512]{1,0:T(8,128)}, u32[]{:S(2)}, u32[]{:S(2)}) collective-permute-start(f32[256,512]{1,0:T(8,128)S(1)} %fusion.4), channel_id=1, source_target_pairs={{0,1},{1,2},{2,3},{4,5},{5,6},{6,7},{8,9},{9,10},{10,11},{12,13},{... | collective-permute-start | bytes 1572872 | tf_op jit(solution)/shard_map/ppermute | solution.py:10
  48.3 90.9 %copy-start.1 = (s32[2048]{0:T(1024)S(1)}, s32[2048]{0:T(1024)}, u32[]{:S(2)}) copy-start(s32[2048]{0:T(1024)} %param.11) | copy-start | bytes 24580
Sparse Core Ops, SparseCore 0:
  139.3 102.5 all-gather.2
where the time goes:
time: 272 us; the launch traced here: 271 us
  matrix products  102 us (38%)
  waiting for transfers between devices  92.8 us (34%)
  local copies, waits for them, and re-layouts  50.7 us (19%)
  between operations  13.5 us (5%)
  starting transfers between devices  10.8 us (4%)
    all_gather x1, waiting for transfers between devices, per_device(): lax.all_gather(part, 'mode', axis=0, tiled=True)  92.8 us
    conv_general_dilated x1, matrix products, depthwise(): lax.conv_general_dilated(signal[None], flipped, (1,), 'VALID', dimension_...  90.9 us
    rev x1, local copies, waits for them, and re-layouts, depthwise(): flipped = jnp.flip(weights, 1)[:, None, :]  11.6 us
    ppermute x4, starting transfers between devices, passed_along(): return lax.ppermute(block, axis, route)  10.7 us
    gather x2, local copies, waits for them, and re-layouts, per_device(): ground = jnp.take(support_accel, groups, axis=0).astype(jnp.float32)  9.92 us
    dot_general x1, matrix products, per_device(): jnp.dot(columns, piece, preferred_element_type=jnp.float32)  9.71 us
    all_gather x1, local copies, waits for them, and re-layouts, per_device(): lax.all_gather(part, 'mode', axis=0, tiled=True)  8.97 us
    broadcast_in_dim x1, local copies, waits for them, and re-layouts, depthwise(): flipped = jnp.flip(weights, 1)[:, None, :]  6.06 us
  transfers between devices with their start and end apart: 5, of which 1 were waited for; matrix products, arithmetic and copies ran while one was open for 12% of the time, Pallas kernels for 0%

commit v1 on v0

--- a/solution.py
+++ b/solution.py
@@ -2,6 +2,23 @@
 import jax.numpy as jnp
 from jax import lax
 from jax.sharding import PartitionSpec as P
+
+
+def laid_out(pieces, dim):
+    pieces = jnp.moveaxis(pieces, 0, dim)
+    shape = pieces.shape
+    return pieces.reshape(*shape[:dim], shape[dim] * shape[dim + 1], *shape[dim + 2 :])
+
+
+def collect(x, axis, dim):
+    peers = lax.axis_size(axis)
+    upward = [(i, (i + 1) % peers) for i in range(peers)]
+    pieces = [x]
+    while len(pieces) < peers:
+        pieces.append(lax.ppermute(pieces[-1], axis, upward))
+    place = lax.axis_index(axis)
+    pieces = jnp.stack(pieces)[(place - jnp.arange(peers)) % peers]
+    return laid_out(pieces, dim)
 
 
 def passed_along(block, axis, distance):
@@ -41,7 +58,7 @@
     window = jnp.concatenate(pieces, axis=1)
     modal = apply_filter(window[:, 1:], masked).astype(jnp.bfloat16)
     initial = jnp.zeros((mode_shapes.shape[0], slab_len), jnp.float32)
-    piece = jax.tree.map(lambda part: lax.all_gather(part, "mode", axis=0, tiled=True), modal)
+    piece = jax.tree.map(lambda part: collect(part, "mode", 0), modal)
     columns = lax.slice_in_dim(mode_shapes, 0, piece.shape[0], axis=1)
     summed = initial + jnp.dot(columns, piece, preferred_element_type=jnp.float32)
     ground = jnp.take(support_accel, groups, axis=0).astype(jnp.float32)

time: 272 us -> 244 us (0.90)
  waiting for transfers between devices: 92.8 us -> 56.3 us
  local copies, waits for them, and re-layouts: 50.7 us -> 71.7 us
  between operations: 13.5 us -> 0.15 us
    all_gather x1 -> x0, waiting for transfers between devices: 92.8 us -> none  [per_device(): lax.all_gather(part, 'mode', axis=0, tiled=True)]
    ppermute x0 -> x7, waiting for transfers between devices: none -> 56.3 us  [collect(): pieces.append(lax.ppermute(pieces[-1], axis, upward))]
    another operation x0 -> x9, local copies, waits for them, and re-layouts: none -> 24.1 us  [collect(): pieces = jnp.stack(pieces)[(place - jnp.arange(peers)) % peers]]
    all_gather x1 -> x0, local copies, waits for them, and re-layouts: 8.97 us -> none  [per_device(): lax.all_gather(part, 'mode', axis=0, tiled=True)]
    gather x0 -> x1, local copies, waits for them, and re-layouts: none -> 3.73 us  [collect(): pieces = jnp.stack(pieces)[(place - jnp.arange(peers)) % peers]]
    unnamed x8 -> x22, local copies, waits for them, and re-layouts: 5.35 us -> 6.8 us
  transfers between devices with their start and end apart: 5 -> 11, of which waited for: 1 -> 6; matrix products, arithmetic and copies ran while one was open for 12% -> 17% of each run, Pallas kernels for 0% -> 0%
where the time goes in v1:
time: 244 us; the launch traced here: 242 us
  matrix products  99.9 us (41%)
  local copies, waits for them, and re-layouts  71.7 us (29%)
  waiting for transfers between devices  56.3 us (23%)
  starting transfers between devices  12.4 us (5%)
    conv_general_dilated x1, matrix products, depthwise(): lax.conv_general_dilated(signal[None], flipped, (1,), 'VALID', dimension_...  88.7 us
    ppermute x7, waiting for transfers between devices, collect(): pieces.append(lax.ppermute(pieces[-1], axis, upward))  56.3 us
    another operation x9, local copies, waits for them, and re-layouts, collect(): pieces = jnp.stack(pieces)[(place - jnp.arange(peers)) % peers]  24.1 us
    rev x1, local copies, waits for them, and re-layouts, depthwise(): flipped = jnp.flip(weights, 1)[:, None, :]  11.6 us
    ppermute x4, starting transfers between devices, passed_along(): return lax.ppermute(block, axis, route)  10.8 us
    gather x2, local copies, waits for them, and re-layouts, per_device(): ground = jnp.take(support_accel, groups, axis=0).astype(jnp.float32)  10 us
    dot_general x1, matrix products, per_device(): jnp.dot(columns, piece, preferred_element_type=jnp.float32)  9.92 us
    unnamed x22, local copies, waits for them, and re-layouts  6.8 us
  transfers between devices with their start and end apart: 11, of which 6 were waited for; matrix products, arithmetic and copies ran while one was open for 17% of the time, Pallas kernels for 0%

profile of v1, /device:TPU:0, one launch (start us, length us, event | category | flops | bytes accessed | tf_op | source)
XLA Modules:
  0.0 242.3 jit_solution(6021438504375579790)
XLA Ops:
  1.0 1.2 fusion.5
  2.3 1.5 collective-permute-start
  3.8 5.1 %collective-permute-start.1 = (f32[256,512]{1,0:T(8,128)S(1)}, f32[256,512]{1,0:T(8,128)}, u32[]{:S(2)}, u32[]{:S(2)}) collective-permute-start(f32[256,512]{1,0:T(8,128)S(1)} %fusion.5), channel_id=1, source_target_pairs={{0,3},{4,7},{8,11},{12,15},{16,19},{20,23},{24,27},{28,31}} | collective-permute-start | bytes 1572872 | tf_op jit(solution)/shard_map/ppermute | solution.py:27
  8.9 2.1 collective-permute-start.2
  11.0 2.1 collective-permute-start.3
  13.1 1.8 fusion.1
  14.9 11.6 %rev.4 = f32[256,2048]{1,0:T(8,128)} reverse(f32[256,2048]{1,0:T(8,128)S(1)} %fusion.1), dimensions={1} | reverse | bytes 4194304 | tf_op jit(solution)/shard_map/jit(_flip)/rev | solution.py:31
  26.5 6.0 %copy.117 = f32[256,1,2048]{0,1,2:T(1,128)} copy(f32[256,1,2048]{2,0,1:T(8,128)} %bitcast.24) | data formatting | bytes 4194304 | tf_op jit(solution)/shard_map/broadcast_in_dim | solution.py:31
  33.7 1.1 constant_dynamic-update-slice_fusion.3
  34.7 1.1 constant_dynamic-update-slice_fusion.2
  35.8 1.1 constant_dynamic-update-slice_fusion.1
  37.7 4.0 %copy.116 = f32[1,256,2559]{1,0,2:T(1,128)} copy(f32[1,256,2559]{2,1,0:T(8,128)S(1)} %slice_bitcast_fusion) | data formatting | bytes 5240832 | tf_op jit(solution)/shard_map/broadcast_in_dim | solution.py:33
  41.7 88.7 %convolution_convert_fusion = bf16[1,256,512]{1,0,2:T(2,128)(2,1)S(1)} fusion(f32[1,256,2559]{1,0,2:T(1,128)} %copy.116, f32[256,1,2048]{0,1,2:T(1,128)} %copy.117), kind=kOutput, calls=%fused_computation.7 | convolution fusion | flops 3221356544 | bytes 4979712 | tf_op jit(solution)/shard_map/conv_general_dilated | solution.py:32
  131.1 1.6 collective-permute-start.4
  132.7 8.6 %collective-permute-done.4 = bf16[256,512]{1,0:T(8,128)(2,1)S(1)} collective-permute-done((bf16[256,512]{1,0:T(8,128)(2,1)S(1)}, bf16[256,512]{1,0:T(8,128)(2,1)S(1)}, u32[]{:S(2)}, u32[]{:S(2)}) %collective-permute-start.4) | collective-permute-done | bytes 262176 | tf_op jit(solution)/shard_map/ppermute | solution.py:18
  141.4 9.3 %collective-permute-done.5 = bf16[256,512]{1,0:T(8,128)(2,1)S(1)} collective-permute-done((bf16[256,512]{1,0:T(8,128)(2,1)S(1)}, bf16[256,512]{1,0:T(8,128)(2,1)S(1)}, u32[]{:S(2)}, u32[]{:S(2)}) %collective-permute-start.5) | collective-permute-done | bytes 262176 | tf_op jit(solution)/shard_map/ppermute | solution.py:18
  151.4 9.1 %collective-permute-done.6 = bf16[256,512]{1,0:T(8,128)(2,1)S(1)} collective-permute-done((bf16[256,512]{1,0:T(8,128)(2,1)S(1)}, bf16[256,512]{1,0:T(8,128)(2,1)S(1)}, u32[]{:S(2)}, u32[]{:S(2)}) %collective-permute-start.6) | collective-permute-done | bytes 262176 | tf_op jit(solution)/shard_map/ppermute | solution.py:18
  161.2 9.1 %collective-permute-done.7 = bf16[256,512]{1,0:T(8,128)(2,1)S(1)} collective-permute-done((bf16[256,512]{1,0:T(8,128)(2,1)S(1)}, bf16[256,512]{1,0:T(8,128)(2,1)S(1)}, u32[]{:S(2)}, u32[]{:S(2)}) %collective-permute-start.7) | collective-permute-done | bytes 262176 | tf_op jit(solution)/shard_map/ppermute | solution.py:18
  170.2 9.7 %collective-permute-done.8 = bf16[256,512]{1,0:T(8,128)(2,1)S(1)} collective-permute-done((bf16[256,512]{1,0:T(8,128)(2,1)S(1)}, bf16[256,512]{1,0:T(8,128)(2,1)S(1)}, u32[]{:S(2)}, u32[]{:S(2)}) %collective-permute-start.8) | collective-permute-done | bytes 262176 | tf_op jit(solution)/shard_map/ppermute | solution.py:18
  180.0 10.6 %collective-permute-done.9 = bf16[256,512]{1,0:T(8,128)(2,1)} collective-permute-done((bf16[256,512]{1,0:T(8,128)(2,1)S(1)}, bf16[256,512]{1,0:T(8,128)(2,1)}, u32[]{:S(2)}, u32[]{:S(2)}) %collective-permute-start.9) | collective-permute-done | bytes 262176 | tf_op jit(solution)/shard_map/ppermute | solution.py:18
  190.6 7.5 %gather_fusion.1 = bf16[2048,512]{1,0:T(8,128)(2,1)S(1)} fusion(bf16[512,512]{1,0:T(8,128)(2,1)S(1)} %copy-done, s32[2048]{0:T(1024)S(1)} %fusion.2), kind=kCustom, calls=%fused_computation.1 | custom fusion | bytes 4202496 | tf_op jit(solution)/shard_map/jit(_take)/gather | solution.py:64
  198.1 2.5 %copy.127 = bf16[2048,512]{0,1:T(8,128)(2,1)} copy(bf16[2048,512]{1,0:T(8,128)(2,1)S(1)} %gather_fusion.1) | data formatting | bytes 4194304 | tf_op jit(solution)/shard_map/jit(_take)/gather | solution.py:64
  200.6 1.1 copy.119
  201.7 1.9 copy.120
  203.6 1.9 copy.121
  207.7 2.0 copy.124
  209.7 1.9 copy.125
  211.6 10.4 %stack.32 = bf16[8,256,512]{1,0,2:T(8,128)(2,1)S(1)} concatenate(bf16[1,256,512]{1,0,2:T(2,128)(2,1)S(1)} %convolution_convert_fusion, bf16[1,256,512]{1,0,2:T(2,128)(2,1)} %copy.119, bf16[1,256,512]{1,0,2:T(2,128)(2,1)} %copy.120, bf16[1,256,512]{1,0,2:T(2,128)(2,1)} %copy.121, bf16[1,256,512]{1,0,2:T(2,128)(2,1)} %copy.122, bf16[1,256,512]{1,0,2:T(2,128)(2,1)} %copy.123, ...), dimensions={0} | concatenate | bytes 4194304 | tf_op jit(solution)/shard_map/stack | solution.py:20
  222.0 2.7 %copy.126 = bf16[8,256,512]{2,1,0:T(8,128)(2,1)} copy(bf16[8,256,512]{1,0,2:T(8,128)(2,1)S(1)} %stack.32) | data formatting | bytes 4194304 | tf_op jit(solution)/shard_map/stack | solution.py:20
  224.7 3.7 %gather_fusion = bf16[8,256,512]{2,1,0:T(8,128)(2,1)} fusion(bf16[8,256,512]{2,1,0:T(8,128)(2,1)} %copy.126, s32[1024]{0:T(1024)S(1)} %pad_clamp_fusion), kind=kCustom, calls=%fused_computation | custom fusion | bytes 4194336 | tf_op jit(solution)/shard_map/gather | solution.py:20
  228.4 9.9 %fusion = bf16[2048,512]{0,1:T(8,128)(2,1)} fusion(bf16[2048,512]{1,0:T(8,128)(2,1)} %bitcast.25, bf16[2048,2048]{1,0:T(8,128)(2,1)} %param.10, bf16[2048,512]{0,1:T(8,128)(2,1)S(1)} %copy-done.1, pred[2048]{0:T(1024)(128)(4,1)S(1)} %compare_and_fusion), kind=kOutput, calls=%fused_computation.3 | convolution fusion | flops 4299161600 | bytes 14682112 | tf_op jit(solution)/shard_map/dot_general | solution.py:63
  238.4 3.9 %copy.128 = bf16[2048,512]{1,0:T(8,128)(2,1)} copy(bf16[2048,512]{0,1:T(8,128)(2,1)} %fusion) | data formatting | bytes 4194304 | tf_op jit(solution)/shard_map/convert_element_type | solution.py:65
  (39 shorter events, 7.2 us)
Async XLA Ops:
  0.0 1.0 copy-start
  2.3 30.3 %collective-permute-start = (f32[256,512]{1,0:T(8,128)S(1)}, f32[256,512]{1,0:T(8,128)}, u32[]{:S(2)}, u32[]{:S(2)}) collective-permute-start(f32[256,512]{1,0:T(8,128)S(1)} %fusion.5), channel_id=1, source_target_pairs={} | collective-permute-start | bytes 1572872 | tf_op jit(solution)/shard_map/ppermute | solution.py:27
  3.8 29.9 %collective-permute-start.1 = (f32[256,512]{1,0:T(8,128)S(1)}, f32[256,512]{1,0:T(8,128)}, u32[]{:S(2)}, u32[]{:S(2)}) collective-permute-start(f32[256,512]{1,0:T(8,128)S(1)} %fusion.5), channel_id=1, source_target_pairs={{0,3},{4,7},{8,11},{12,15},{16,19},{20,23},{24,27},{28,31}} | collective-permute-start | bytes 1572872 | tf_op jit(solution)/shard_map/ppermute | solution.py:27
  8.9 25.9 %collective-permute-start.2 = (f32[256,512]{1,0:T(8,128)S(1)}, f32[256,512]{1,0:T(8,128)}, u32[]{:S(2)}, u32[]{:S(2)}) collective-permute-start(f32[256,512]{1,0:T(8,128)S(1)} %fusion.5), channel_id=1, source_target_pairs={{0,2},{1,3},{4,6},{5,7},{8,10},{9,11},{12,14},{13,15},{16,18},{17,... | collective-permute-start | bytes 1572872 | tf_op jit(solution)/shard_map/ppermute | solution.py:27
  11.0 24.9 %collective-permute-start.3 = (f32[256,512]{1,0:T(8,128)S(1)}, f32[256,512]{1,0:T(8,128)}, u32[]{:S(2)}, u32[]{:S(2)}) collective-permute-start(f32[256,512]{1,0:T(8,128)S(1)} %fusion.5), channel_id=1, source_target_pairs={{0,1},{1,2},{2,3},{4,5},{5,6},{6,7},{8,9},{9,10},{10,11},{12,13},{... | collective-permute-start | bytes 1572872 | tf_op jit(solution)/shard_map/ppermute | solution.py:27
  41.7 138.2 %copy-start.8 = (s32[2048]{0:T(1024)S(1)}, s32[2048]{0:T(1024)}, u32[]{:S(2)}) copy-start(s32[2048]{0:T(1024)} %param.11) | copy-start | bytes 24580
  131.1 10.2 %collective-permute-start.4 = (bf16[256,512]{1,0:T(8,128)(2,1)S(1)}, bf16[256,512]{1,0:T(8,128)(2,1)S(1)}, u32[]{:S(2)}, u32[]{:S(2)}) collective-permute-start(bf16[256,512]{1,0:T(8,128)(2,1)S(1)} %bitcast.31), channel_id=1, source_target_pairs={{0,4},{4,8},{8,12},{12,16},{16,20},{20,24},{24,28},{28,0},{1,5},{5... | collective-permute-start | bytes 786440 | tf_op jit(solution)/shard_map/ppermute | solution.py:18
  141.4 9.3 %collective-permute-start.5 = (bf16[256,512]{1,0:T(8,128)(2,1)S(1)}, bf16[256,512]{1,0:T(8,128)(2,1)S(1)}, u32[]{:S(2)}, u32[]{:S(2)}) collective-permute-start(bf16[256,512]{1,0:T(8,128)(2,1)S(1)} %collective-permute-done.4), channel_id=1, source_target_pairs={{0,4},{4,8},{8,12},{12,16},{16,20},{20,24},{24,28},{28,0},{1,5},{5... | collective-permute-start | bytes 786440 | tf_op jit(solution)/shard_map/ppermute | solution.py:18
  150.7 0.7 copy-start.2
  151.4 9.1 %collective-permute-start.6 = (bf16[256,512]{1,0:T(8,128)(2,1)S(1)}, bf16[256,512]{1,0:T(8,128)(2,1)S(1)}, u32[]{:S(2)}, u32[]{:S(2)}) collective-permute-start(bf16[256,512]{1,0:T(8,128)(2,1)S(1)} %collective-permute-done.5), channel_id=1, source_target_pairs={{0,4},{4,8},{8,12},{12,16},{16,20},{20,24},{24,28},{28,0},{1,5},{5... | collective-permute-start | bytes 786440 | tf_op jit(solution)/shard_map/ppermute | solution.py:18
  160.5 0.7 copy-start.3
  161.2 9.1 %collective-permute-start.7 = (bf16[256,512]{1,0:T(8,128)(2,1)S(1)}, bf16[256,512]{1,0:T(8,128)(2,1)S(1)}, u32[]{:S(2)}, u32[]{:S(2)}) collective-permute-start(bf16[256,512]{1,0:T(8,128)(2,1)S(1)} %collective-permute-done.6), channel_id=1, source_target_pairs={{0,4},{4,8},{8,12},{12,16},{16,20},{20,24},{24,28},{28,0},{1,5},{5... | collective-permute-start | bytes 786440 | tf_op jit(solution)/shard_map/ppermute | solution.py:18
  170.2 20.3 %copy-start.4 = (bf16[256,512]{1,0:T(8,128)(2,1)}, bf16[256,512]{1,0:T(8,128)(2,1)S(1)}, u32[]{:S(2)}) copy-start(bf16[256,512]{1,0:T(8,128)(2,1)S(1)} %collective-permute-done.7) | copy-start | bytes 786436
  170.2 9.7 %collective-permute-start.8 = (bf16[256,512]{1,0:T(8,128)(2,1)S(1)}, bf16[256,512]{1,0:T(8,128)(2,1)S(1)}, u32[]{:S(2)}, u32[]{:S(2)}) collective-permute-start(bf16[256,512]{1,0:T(8,128)(2,1)S(1)} %collective-permute-done.7), channel_id=1, source_target_pairs={{0,4},{4,8},{8,12},{12,16},{16,20},{20,24},{24,28},{28,0},{1,5},{5... | collective-permute-start | bytes 786440 | tf_op jit(solution)/shard_map/ppermute | solution.py:18
  179.9 10.6 %copy-start.6 = (bf16[256,512]{1,0:T(8,128)(2,1)}, bf16[256,512]{1,0:T(8,128)(2,1)S(1)}, u32[]{:S(2)}) copy-start(bf16[256,512]{1,0:T(8,128)(2,1)S(1)} %collective-permute-done.8) | copy-start | bytes 786436
  179.9 10.6 %collective-permute-start.9 = (bf16[256,512]{1,0:T(8,128)(2,1)S(1)}, bf16[256,512]{1,0:T(8,128)(2,1)}, u32[]{:S(2)}, u32[]{:S(2)}) collective-permute-start(bf16[256,512]{1,0:T(8,128)(2,1)S(1)} %collective-permute-done.8), channel_id=1, source_target_pairs={{0,4},{4,8},{8,12},{12,16},{16,20},{20,24},{24,28},{28,0},{1,5},{5... | collective-permute-start | bytes 786440 | tf_op jit(solution)/shard_map/ppermute | solution.py:18
  190.5 19.1 %collective-permute-start.10 = (bf16[256,512]{1,0:T(8,128)(2,1)}, bf16[256,512]{1,0:T(8,128)(2,1)}, u32[]{:S(2)}, u32[]{:S(2)}) collective-permute-start(bf16[256,512]{1,0:T(8,128)(2,1)} %collective-permute-done.9), channel_id=1, source_target_pairs={{0,4},{4,8},{8,12},{12,16},{16,20},{20,24},{24,28},{28,0},{1,5},{5... | collective-permute-start | bytes 786440 | tf_op jit(solution)/shard_map/ppermute | solution.py:18
  200.6 5.0 %copy-start.5 = (bf16[256,512]{1,0:T(8,128)(2,1)S(1)}, bf16[256,512]{1,0:T(8,128)(2,1)}, u32[]{:S(2)}) copy-start(bf16[256,512]{1,0:T(8,128)(2,1)} %copy-done.4) | copy-start | bytes 786436
  200.6 6.0 %copy-start.7 = (bf16[256,512]{1,0:T(8,128)(2,1)S(1)}, bf16[256,512]{1,0:T(8,128)(2,1)}, u32[]{:S(2)}) copy-start(bf16[256,512]{1,0:T(8,128)(2,1)} %copy-done.6) | copy-start | bytes 786436
  224.7 3.7 %copy-start.1 = (bf16[2048,512]{0,1:T(8,128)(2,1)S(1)}, bf16[2048,512]{0,1:T(8,128)(2,1)}, u32[]{:S(2)}) copy-start(bf16[2048,512]{0,1:T(8,128)(2,1)} %copy.127) | copy-start | bytes 6291460
